TPU v7x, 32 devices: a whole 2x2x4 slice. The times are simulated.
32 devices in a mesh: groups: 2 (over y), pfx: 4 (over z), smp: 2 (over x), kv: 2 (over core).
Axes of the slice: x: 2, y: 2, z: 4, core: 2. Of those that a mesh axis runs over, the one named last changes fastest.
Arguments:
- hidden: bfloat16 [64, 8192], P(('groups', 'smp'), 'pfx'), parts along dimension 0, may hold values from -6 to 6
- norm_gain: bfloat16 [8192], P('pfx'), may hold values from 0.5 to 1.5
- query_weight: bfloat16 [8192, 4096], P('pfx', 'kv'), may hold values from -0.0625 to 0.0625
- key_matrix: bfloat16 [8192, 512], P('pfx', 'kv'), may hold values from -0.52734375 to 0.52734375
- value_matrix: bfloat16 [8192, 512], P('pfx', 'kv'), may hold values from -0.0625 to 0.0625
- prefix_key: bfloat16 [16384, 512], P(('groups', 'pfx', 'smp'), 'kv'), parts along dimension 0, may hold values from -160 to 160
- shared_prefix_value: bfloat16 [16384, 512], P(('groups', 'pfx', 'smp'), 'kv'), parts along dimension 0, may hold values from -6 to 6
- sample_suffix_key: bfloat16 [64, 128, 512], P(('groups', 'smp'), 'pfx', 'kv'), parts along dimension 0, may hold values from -24 to 24
- sample_suffix_value: bfloat16 [64, 128, 512], P(('groups', 'smp'), 'pfx', 'kv'), parts along dimension 0, may hold values from -6 to 6
- lengths: int32 [64], P(('groups', 'smp')), parts along dimension 0, may hold values from 1 to 128, as said below
- assign: int32 [64], P(('groups', 'smp')), parts along dimension 0, may hold values from 0 to 31, as said below
Outputs:
- attended: bfloat16 [64, 4096], P(('groups', 'smp'), 'kv'), parts along dimension 0
There are 2 independent parts, one for each index of `groups`. A program takes and returns all parts, laid end to end along the dimension named above; an argument that names none is the same for every part. Nothing has to cross between parts.
Inputs may be any that keep to these rules, and one draw needn't show every extreme that they name: `lengths`: some sample has exactly 128 live positions. `assign`: each aligned block of 16 rows holds each sample number of that block once.
All inputs are finite; a program needn't handle non-finite values.
Results may differ from a plain program's by a relative error of at most 0.017.
Values may be sent and summed in bfloat16 or wider, within the bound.
No kernel may reach another device: no remote copies, remote signals or barrier semaphores. Data moves between devices by JAX's collectives and lax.ppermute only.
A program may use at most 64 MiB of HBM per device.

v0:
```python
import jax
import jax.numpy as jnp
from jax import lax
from jax.sharding import PartitionSpec as P

MODEL_WIDTH = 8192
HEAD_WIDTH = 128


norm_eps = 1e-05
very_negative = -1e30


def prefix_head(operands):
    query_block, key_block, value_block = operands
    scores = jnp.einsum(
        "bgd,kd->bgk", query_block, key_block, preferred_element_type=jnp.float32
    ) * HEAD_WIDTH ** (-0.5)
    top_score = jnp.max(scores, axis=2)
    weights = jnp.exp(scores - top_score[..., None]).astype(jnp.bfloat16)
    denominator = jnp.sum(weights.astype(jnp.float32), axis=2)
    numerator = jnp.einsum("bgk,kd->bgd", weights, value_block, preferred_element_type=jnp.float32)
    return (numerator, denominator, top_score)


def body(
    hidden,
    norm_gain,
    query_weight,
    key_matrix,
    value_matrix,
    prefix_key,
    shared_prefix_value,
    sample_suffix_key,
    sample_suffix_value,
    lengths,
    assign,
):
    local_rows = hidden.shape[0]
    local_kv = key_matrix.shape[1] // HEAD_WIDTH
    local_heads = query_weight.shape[1] // HEAD_WIDTH
    group_width = local_heads // local_kv
    score_scale = HEAD_WIDTH ** (-0.5)
    hidden_wide = hidden.astype(jnp.float32)
    normed = (hidden_wide * norm_gain.astype(jnp.float32)).astype(jnp.bfloat16)
    query_part = jnp.dot(normed, query_weight, preferred_element_type=jnp.float32)
    key_part = jnp.dot(normed, key_matrix, preferred_element_type=jnp.float32)
    value_part = jnp.dot(normed, value_matrix, preferred_element_type=jnp.float32)
    square_part = jnp.sum(hidden_wide * hidden_wide, axis=1)
    query_sum, key_sum, value_sum, square_sum = lax.psum(
        (query_part, key_part, value_part, square_part), "pfx"
    )
    rms_value = jnp.sqrt(square_sum / MODEL_WIDTH + norm_eps)
    query_rows = (query_sum / rms_value[:, None]).astype(jnp.bfloat16)
    new_key = (key_sum / rms_value[:, None]).astype(jnp.bfloat16)
    new_value = (value_sum / rms_value[:, None]).astype(jnp.bfloat16)
    all_queries = lax.all_gather(query_rows, "smp", axis=0, tiled=True)
    sample_count = all_queries.shape[0]
    head_queries = jnp.transpose(
        all_queries.reshape(sample_count, local_kv, group_width, HEAD_WIDTH), (1, 0, 2, 3)
    )
    head_keys = jnp.transpose(prefix_key.reshape(-1, local_kv, HEAD_WIDTH), (1, 0, 2))
    head_values = jnp.transpose(shared_prefix_value.reshape(-1, local_kv, HEAD_WIDTH), (1, 0, 2))
    pre_numer, pre_denom, pre_top = lax.map(prefix_head, (head_queries, head_keys, head_values))
    pre_numer = jnp.transpose(pre_numer, (1, 0, 2, 3)).reshape(
        sample_count, local_heads, HEAD_WIDTH
    )
    pre_denom = jnp.transpose(pre_denom, (1, 0, 2)).reshape(sample_count, local_heads)
    pre_top = jnp.transpose(pre_top, (1, 0, 2)).reshape(sample_count, local_heads)
    row_base = lax.axis_index("smp") * local_rows
    slot_index = assign - row_base
    one_hot = (slot_index[:, None] == jnp.arange(local_rows, dtype=jnp.int32)[None, :]).astype(
        jnp.float32
    )
    slot_query = jnp.einsum(
        "rs,rx->sx", one_hot, query_rows.astype(jnp.float32), precision=lax.Precision.HIGHEST
    ).astype(jnp.bfloat16)
    slot_query = slot_query.reshape(local_rows, local_kv, group_width, HEAD_WIDTH)
    suffix_len = sample_suffix_key.shape[1]
    suffix_keys = sample_suffix_key.reshape(local_rows, suffix_len, local_kv, HEAD_WIDTH)
    suffix_values = sample_suffix_value.reshape(local_rows, suffix_len, local_kv, HEAD_WIDTH)
    suffix_scores = (
        jnp.einsum("shgd,sthd->shgt", slot_query, suffix_keys, preferred_element_type=jnp.float32)
        * score_scale
    )
    position = lax.axis_index("pfx") * suffix_len + jnp.arange(suffix_len, dtype=jnp.int32)
    live_mask = (position[None, :] < lengths[:, None])[:, None, None, :]
    suffix_scores = jnp.where(live_mask, suffix_scores, very_negative)
    suffix_top = jnp.max(suffix_scores, axis=3)
    suffix_weights = jnp.where(
        live_mask, jnp.exp(suffix_scores - suffix_top[..., None]), 0.0
    ).astype(jnp.bfloat16)
    suffix_denom = jnp.sum(suffix_weights.astype(jnp.float32), axis=3)
    suffix_numer = jnp.einsum(
        "shgt,sthd->shgd", suffix_weights, suffix_values, preferred_element_type=jnp.float32
    )
    row_numer = jnp.einsum(
        "rs,shgd->rhgd", one_hot, suffix_numer, precision=lax.Precision.HIGHEST
    ).reshape(local_rows, local_heads, HEAD_WIDTH)
    row_denom = jnp.einsum(
        "rs,shg->rhg", one_hot, suffix_denom, precision=lax.Precision.HIGHEST
    ).reshape(local_rows, local_heads)
    row_top = jnp.einsum(
        "rs,shg->rhg", one_hot, suffix_top, precision=lax.Precision.HIGHEST
    ).reshape(local_rows, local_heads)
    full_top = lax.dynamic_update_slice(
        jnp.full((sample_count, local_heads), very_negative, jnp.float32), row_top, (row_base, 0)
    )
    local_top = jnp.maximum(pre_top, full_top)
    global_top = lax.pmax(local_top, ("pfx", "smp"))
    own_top = lax.dynamic_slice_in_dim(global_top, row_base, local_rows, 0)
    pre_factor = jnp.exp(pre_top - global_top)
    row_factor = jnp.exp(row_top - own_top)
    scaled_row_numer = row_numer * row_factor[..., None]
    scaled_row_denom = row_denom * row_factor
    term_numer = pre_numer * pre_factor[..., None]
    term_denom = pre_denom * pre_factor
    term_numer = lax.dynamic_update_slice(
        term_numer,
        lax.dynamic_slice_in_dim(term_numer, row_base, local_rows, 0) + scaled_row_numer,
        (row_base, 0, 0),
    )
    term_denom = lax.dynamic_update_slice(
        term_denom,
        lax.dynamic_slice_in_dim(term_denom, row_base, local_rows, 0) + scaled_row_denom,
        (row_base, 0),
    )
    block_numer, block_denom = (
        lax.psum_scatter(
            term_numer.astype(jnp.bfloat16), "smp", scatter_dimension=0, tiled=True
        ).astype(jnp.float32),
        lax.psum_scatter(
            term_denom.astype(jnp.bfloat16), "smp", scatter_dimension=0, tiled=True
        ).astype(jnp.float32),
    )
    numerator, denominator = (
        lax.psum(block_numer.astype(jnp.bfloat16), "pfx").astype(jnp.float32),
        lax.psum(block_denom.astype(jnp.bfloat16), "pfx").astype(jnp.float32),
    )
    query_wide = query_rows.reshape(local_rows, local_kv, group_width, HEAD_WIDTH).astype(
        jnp.float32
    )
    own_key = new_key.reshape(local_rows, local_kv, 1, HEAD_WIDTH).astype(jnp.float32)
    own_score = (jnp.sum(query_wide * own_key, axis=3) * score_scale).reshape(
        local_rows, local_heads
    )
    final_top = jnp.maximum(own_top, own_score)
    old_factor = jnp.exp(own_top - final_top)
    own_weight = lax.optimization_barrier(
        jnp.exp(own_score - final_top).astype(jnp.bfloat16)
    ).astype(jnp.float32)
    own_value = jnp.broadcast_to(
        new_value.reshape(local_rows, local_kv, 1, HEAD_WIDTH).astype(jnp.float32),
        (local_rows, local_kv, group_width, HEAD_WIDTH),
    ).reshape(local_rows, local_heads, HEAD_WIDTH)
    numerator = numerator * old_factor[..., None] + own_weight[..., None] * own_value
    denominator = denominator * old_factor + own_weight
    return (
        (numerator / denominator[..., None])
        .astype(jnp.bfloat16)
        .reshape(local_rows, local_heads * HEAD_WIDTH)
    )


def solution(mesh):
    return jax.shard_map(
        body,
        mesh=mesh,
        in_specs=(
            P(("groups", "smp"), "pfx"),
            P("pfx"),
            P("pfx", "kv"),
            P("pfx", "kv"),
            P("pfx", "kv"),
            P(("groups", "pfx", "smp"), "kv"),
            P(("groups", "pfx", "smp"), "kv"),
            P(("groups", "smp"), "pfx", "kv"),
            P(("groups", "smp"), "pfx", "kv"),
            P(("groups", "smp")),
            P(("groups", "smp")),
        ),
        out_specs=P(("groups", "smp"), "kv"),
        check_vma=False,
    )
```

profile of v0, /device:TPU:0, one launch (start us, length us, event | category | flops | bytes accessed | tf_op | source)
XLA Modules:
  0.0 151.5 jit_solution(18185746916683848563)
XLA Ops:
  6.5 0.8 convert_element_type.89
  7.4 5.4 %fusion.30 = f32[16,2048]{1,0:T(8,128)} fusion(bf16[2048,2048]{1,0:T(8,128)(2,1)} %param.15, bf16[16,2048]{1,0:T(8,128)(2,1)} %param.13, f32[2048]{0:T(1024)S(1)} %convert_element_type.89), kind=kOutput, calls=%fused_computation.49 | convolution fusion | flops 134316032 | bytes 8593408 | tf_op jit(solution)/shard_map/dot_general | solution.py:46
  12.9 0.1 fusion.18
  13.0 0.5 iota_add_fusion
  13.5 0.2 fusion.28
  13.8 0.3 fusion.26
  14.0 21.5 %all-reduce = (f32[16]{0:T(128)S(1)}, f32[16,256]{1,0:T(8,128)S(1)}, f32[16,256]{1,0:T(8,128)S(1)}) all-reduce(f32[16]{0:T(128)S(1)} %fusion.18, f32[16,256]{1,0:T(8,128)S(1)} %fusion.28, f32[16,256]{1,0:T(8,128)S(1)} %fusion.26), channel_id=1, replica_groups=mesh['groups'=2,'pfx'=4,'smp'=2,'kv'=2] {'pfx'}, use_global_device_ids=true, to_apply=%region_2.0 | all-reduce | flops 8208 | bytes 65664 | tf_op jit(solution)/shard_map/psum | solution.py:50
  35.7 0.2 copy.55
  35.9 0.2 copy.56
  36.1 0.7 broadcast_compare_fusion
  36.8 0.7 broadcast_subtract_fusion
  37.4 13.1 %all-reduce.4.cloned.1.call-done = f32[16,2048]{1,0:T(8,128)} async-done(((f32[16,2048]{1,0:T(8,128)}), f32[16,2048]{1,0:T(8,128)}) %all-reduce.4.cloned.1.call-update) | async-done | bytes 131088 | tf_op jit(solution)/shard_map/psum | solution.py:50
  50.5 1.0 convert_bitcast_fusion
  51.5 0.1 multiply_reduce_fusion
  51.7 4.9 %all_gather.3 = bf16[32,2048]{1,0:T(8,128)(2,1)S(1)} all-gather(bf16[16,2048]{1,0:T(8,128)(2,1)S(1)} %get-tuple-element.97), channel_id=1, replica_groups=mesh['groups'=2,'pfx'=4,'smp'=2,'kv'=2] {'smp'}, dimensions={0}, use_global_device_ids=true | all-gather | bytes 196608 | tf_op jit(solution)/shard_map/all_gather | solution.py:57
  56.7 0.3 fusion.10
  57.0 0.3 fusion.51
  57.4 0.2 fusion.38
  57.6 0.2 convert_reduce_fusion.1
  57.9 1.2 fusion.12
  59.1 0.3 fusion.24
  59.4 4.6 %while.14 = (s32[]{:T(128)}, f32[2,32,8,128]{3,2,0,1:T(8,128)}, f32[2,32,8]{2,1,0:T(8,128)}, f32[2,32,8]{2,1,0:T(8,128)S(1)}, bf16[2,32,8,128]{3,2,1,0:T(8,128)(...) while((s32[]{:T(128)}, f32[2,32,8,128]{3,2,0,1:T(8,128)}, ...), condition=%wide.region_6.7_spmd, body=%wide.region_3.6_spmd.sunk | while | flops 136314368 | bytes 3953761 | solution.py:64
  59.4 0.4 fusion.63
  59.8 0.3 convert_reduce_fusion.3
  60.1 1.0 fusion.64
  61.1 0.6 bitcast_dynamic-update-slice_fusion.3
  61.7 0.4 fusion.63
  62.1 0.3 convert_reduce_fusion.3
  62.4 1.0 fusion.64
  63.4 0.6 bitcast_dynamic-update-slice_fusion.3
  64.1 0.2 dynamic_update_slice.20
  64.3 20.4 %pmax.7 = f32[32,16]{0,1:T(8,128)S(1)} all-reduce(f32[32,16]{0,1:T(8,128)S(1)} %bitcast_maximum_fusion), channel_id=1, replica_groups=mesh['groups'=2,'pfx'=4,'smp'=2,'kv'=2] {'pfx','smp'}, use_global_device_ids=true, to_apply=%region_8.9 | all-reduce | flops 512 | bytes 4096 | tf_op jit(solution)/shard_map/pmax | solution.py:110
  84.7 0.1 fusion.34
  84.9 0.8 copy.71
  85.7 0.2 fusion.11
  85.9 0.2 dynamic_update_slice.22
  86.1 0.7 copy.75
  86.9 1.1 bitcast_multiply_fusion
  88.0 0.1 fusion.23
  88.1 0.7 convert_element_type.94
  88.9 5.2 %reduce-scatter.7.cloned.1.call-done = bf16[16,16]{1,0:T(8,128)(2,1)} async-done(((bf16[32,16]{1,0:T(8,128)(2,1)}), bf16[16,16]{1,0:T(8,128)(2,1)}) %reduce-scatter.7.cloned.1.call-update) | async-done | bytes 528
  94.2 0.7 copy.76
  94.9 11.7 %psum.47 = bf16[16,16]{0,1:T(8,128)(2,1)S(1)} all-reduce(bf16[16,16]{0,1:T(8,128)(2,1)S(1)} %copy.76), channel_id=1, replica_groups=mesh['groups'=2,'pfx'=4,'smp'=2,'kv'=2] {'pfx'}, use_global_device_ids=true, to_apply=%region_16.17 | all-reduce | flops 256 | bytes 1024 | tf_op jit(solution)/shard_map/psum | solution.py:138
  106.6 0.2 reduce-scatter.5.cloned.1.call-done
  106.8 0.1 multiply_add_fusion
  107.0 36.3 %all-reduce.6.cloned.1.call-done = bf16[16,16,128]{2,1,0:T(8,128)(2,1)} async-done(((bf16[16,16,128]{2,1,0:T(8,128)(2,1)}), bf16[16,16,128]{2,1,0:T(8,128)(2,1)}) %all-reduce.6.cloned.1.call-update) | async-done | bytes 65552 | tf_op jit(solution)/shard_map/psum | solution.py:137
  143.3 1.0 fusion.21
  144.3 0.6 copy.110
  (46 shorter events, 1.1 us)
Async XLA Ops:
  6.5 7.0 %copy-start = (bf16[2048,256]{1,0:T(8,128)(2,1)S(1)}, bf16[2048,256]{1,0:T(8,128)(2,1)}, u32[]{:S(2)}) copy-start(bf16[2048,256]{1,0:T(8,128)(2,1)} %param.16) | copy-start | bytes 3145732
  6.5 6.3 %copy-start.1 = (bf16[16,2048]{1,0:T(8,128)(2,1)S(1)}, bf16[16,2048]{1,0:T(8,128)(2,1)}, u32[]{:S(2)}) copy-start(bf16[16,2048]{1,0:T(8,128)(2,1)} %param.13) | copy-start | bytes 196612
  6.5 44.0 %all-reduce.4.cloned.1.call-start = ((), (), s32[]{:S(2)}) async-start(), calls=%async_computation.2 | async-start | bytes 262144 | tf_op jit(solution)/shard_map/psum | solution.py:50
  7.3 6.5 %copy-start.2 = (bf16[2048,256]{1,0:T(8,128)(2,1)S(1)}, bf16[2048,256]{1,0:T(8,128)(2,1)}, u32[]{:S(2)}) copy-start(bf16[2048,256]{1,0:T(8,128)(2,1)} %param.17) | copy-start | bytes 3145732
  7.3 28.3 %copy-start.3 = (bf16[1024,256]{1,0:T(8,128)(2,1)S(1)}, bf16[1024,256]{1,0:T(8,128)(2,1)}, u32[]{:S(2)}) copy-start(bf16[1024,256]{1,0:T(8,128)(2,1)} %param.18) | copy-start | bytes 1572868
  7.3 28.5 %copy-start.4 = (bf16[1024,256]{1,0:T(8,128)(2,1)S(1)}, bf16[1024,256]{1,0:T(8,128)(2,1)}, u32[]{:S(2)}) copy-start(bf16[1024,256]{1,0:T(8,128)(2,1)} %param.19) | copy-start | bytes 1572868
  7.3 28.8 %copy-start.6 = (s32[16]{0:T(128)S(1)}, s32[16]{0:T(128)}, u32[]{:S(2)}) copy-start(s32[16]{0:T(128)} %param.22) | copy-start | bytes 196
  7.3 49.7 %copy-start.5 = (bf16[16,32,256]{2,1,0:T(8,128)(2,1)S(1)}, bf16[16,32,256]{2,1,0:T(8,128)(2,1)}, u32[]{:S(2)}) copy-start(bf16[16,32,256]{2,1,0:T(8,128)(2,1)} %param.20) | copy-start | bytes 786436
  12.8 81.4 %reduce-scatter.7.cloned.1.call-start = ((), (), s32[]{:S(2)}) async-start(), calls=%async_computation.5 | async-start | bytes 12288
  86.8 20.0 %reduce-scatter.5.cloned.1.call-start = ((), (), s32[]{:S(2)}) async-start(), calls=%async_computation.3 | async-start | bytes 196608 | tf_op jit(solution)/shard_map/reduce_scatter | solution.py:129
  88.8 54.5 %all-reduce.6.cloned.1.call-start = ((), (), s32[]{:S(2)}) async-start(), calls=%async_computation.4 | async-start | bytes 131072 | tf_op jit(solution)/shard_map/psum | solution.py:137
Sparse Core Ops, SparseCore 0:
  12.9 37.5 all-reduce.3
  86.9 7.2 reduce-scatter.6
  96.4 10.3 reduce-scatter.4
  109.0 34.2 all-reduce.5
where the time goes:
time: 152 us; the launch traced here: 151 us
  blocking collectives  58.5 us (38%)
  waiting for transfers between devices  54.8 us (36%)
  between operations  13.4 us (9%)
  matrix products  11.1 us (7%)
  other arithmetic  7.82 us (5%)
  local copies, waits for them, and re-layouts  5.69 us (4%)
    psum x1, waiting for transfers between devices, body(): lax.psum(block_numer.astype(jnp.bfloat16), 'pfx').astype(jnp.float32)  36.3 us
    psum x1, blocking collectives, body(): lax.psum((query_part, key_part, value_part, square_part), 'pfx')  21.5 us
    pmax x1, blocking collectives, body(): global_top = lax.pmax(local_top, ('pfx', 'smp'))  20.4 us
    psum x1, waiting for transfers between devices, body(): lax.psum((query_part, key_part, value_part, square_part), 'pfx')  13.1 us
    psum x1, blocking collectives, body(): lax.psum(block_denom.astype(jnp.bfloat16), 'pfx').astype(jnp.float32)  11.7 us
    dot_general x1, matrix products, body(): jnp.dot(normed, query_weight, preferred_element_type=jnp.float32)  5.42 us
    unnamed x5, waiting for transfers between devices  5.3 us
    all_gather x1, blocking collectives, body(): all_queries = lax.all_gather(query_rows, 'smp', axis=0, tiled=True)  4.93 us
  transfers between devices with their start and end apart: 4, of which 4 were waited for; matrix products, arithmetic and copies ran while one was open for 4% of the time, Pallas kernels for 0%

commit v1 on v0

v1 whole, which is shorter than its diff:
```python
import jax
import jax.numpy as jnp
from jax import lax
from jax.experimental import pallas as pl
from jax.experimental.pallas import tpu as pltpu
from jax.sharding import PartitionSpec as P

HEAD_WIDTH = 128
LANES = 128
norm_eps = 1e-05
very_negative = -1e30
score_scale = HEAD_WIDTH ** (-0.5)
bf16 = jnp.bfloat16
f32 = jnp.float32

ANY = pl.BlockSpec(memory_space=pl.ANY)
VMEM = pl.BlockSpec(memory_space=pltpu.VMEM)
SMEM = pl.BlockSpec(memory_space=pltpu.SMEM)


def start_copies(sources, targets, sems):
    copies = [
        pltpu.make_async_copy(source, target, sems.at[place])
        for place, (source, target) in enumerate(zip(sources, targets))
    ]
    for copy in copies:
        copy.start()
    return copies


def project(hidden, norm_gain, query_weight, key_matrix, value_matrix, chunks):
    rows, width = hidden.shape
    query_width = query_weight.shape[1]
    kv_width = key_matrix.shape[1]
    total = query_width + 2 * kv_width + LANES
    depth = width // chunks

    def kernel(hidden_in, gain_in, wq_in, wk_in, wv_in, out, hidden_v, gain_v, wq, wk, wv, sems):
        small = start_copies((hidden_in, gain_in), (hidden_v, gain_v), sems)
        large = []
        for chunk in range(chunks):
            part = pl.ds(chunk * depth, depth)
            large.append(
                start_copies(
                    (wq_in.at[part], wk_in.at[part], wv_in.at[part]),
                    (wq.at[part], wk.at[part], wv.at[part]),
                    sems.at[pl.ds(2 + 3 * chunk, 3)],
                )
            )
        for copy in small:
            copy.wait()
        wide = hidden_v[...].astype(f32)
        squares = jnp.sum(wide * wide, axis=1, keepdims=True)
        out[:, query_width + 2 * kv_width :] = jnp.broadcast_to(squares, (rows, LANES))
        normed = (wide * gain_v[...].astype(f32)).astype(bf16)
        for chunk in range(chunks):
            for copy in large[chunk]:
                copy.wait()
            part = pl.ds(chunk * depth, depth)
            left = normed[:, chunk * depth : (chunk + 1) * depth]
            place = 0
            for weight in (wq, wk, wv):
                columns = weight.shape[1]
                value = jnp.dot(left, weight[part], preferred_element_type=f32)
                if chunk == 0:
                    out[:, place : place + columns] = value
                else:
                    out[:, place : place + columns] += value
                place += columns

    return pl.pallas_call(
        kernel,
        in_specs=[ANY] * 5,
        out_specs=VMEM,
        out_shape=jax.ShapeDtypeStruct((rows, total), f32),
        scratch_shapes=[
            pltpu.VMEM(hidden.shape, bf16),
            pltpu.VMEM((1, width), bf16),
            pltpu.VMEM(query_weight.shape, bf16),
            pltpu.VMEM(key_matrix.shape, bf16),
            pltpu.VMEM(value_matrix.shape, bf16),
            pltpu.SemaphoreType.DMA((2 + 3 * chunks,)),
        ],
        compiler_params=pltpu.CompilerParams(vmem_limit_bytes=60 << 20),
        cost_estimate=pl.CostEstimate(
            flops=2 * rows * width * total, bytes_accessed=2 * width * total, transcendentals=0
        ),
        name="project",
    )(hidden, norm_gain.reshape(1, width), query_weight, key_matrix, value_matrix)


def scores_of(queries, keys):
    return (
        lax.dot_general(queries, keys, (((1,), (1,)), ((), ())), preferred_element_type=f32)
        * score_scale
    )


def own_attention(parts, keys, values, suffix_keys, suffix_values, lengths, assign, sizes):
    rows, query_width, kv_width, model_width, suffix_len = sizes
    kv_heads = kv_width // HEAD_WIDTH
    group = query_width // kv_width
    tall = group * rows
    count = len(parts)
    prefix = keys.shape[0]
    suffix = suffix_keys.shape[0]

    def kernel(*refs):
        part_in = refs[:count]
        k_in, v_in, ks_in, vs_in, len_s, assign_s = refs[count : count + 6]
        q_out, acc_out, top_out, sum_out = refs[count + 6 : count + 10]
        part_v, k_v, v_v, ks_v, vs_v, sems = refs[count + 10 :]
        copies = start_copies(
            (*part_in, k_in, ks_in, v_in, vs_in),
            (*(part_v.at[i] for i in range(count)), k_v, ks_v, v_v, vs_v),
            sems,
        )
        first = lax.axis_index("pfx") == 0
        row_base = lax.axis_index("smp") * rows
        position_base = lax.axis_index("pfx") * suffix_len
        slot_of = lax.broadcasted_iota(jnp.int32, (rows, suffix), 1) // suffix_len
        place_of = lax.broadcasted_iota(jnp.int32, (rows, suffix), 1) % suffix_len + position_base
        row_of = lax.broadcasted_iota(jnp.int32, (rows, suffix), 0)
        live_len = jnp.zeros((rows, suffix), jnp.int32)
        row_slot = jnp.zeros((rows, suffix), jnp.int32)
        for i in range(rows):
            live_len = jnp.where(slot_of == i, len_s[i], live_len)
            row_slot = jnp.where(row_of == i, assign_s[i] - row_base, row_slot)
        live = (slot_of == row_slot) & (place_of < live_len)
        bias = jnp.where(live, 0.0, very_negative)
        bias = jnp.concatenate([bias] * group, axis=0)
        for copy in copies[:count]:
            copy.wait()
        total = part_v[0]
        for i in range(1, count):
            total = total + part_v[i]
        squares = total[:, query_width + 2 * kv_width :][:, :1]
        rms = jnp.sqrt(squares / model_width + norm_eps)
        projected = (total[:, : query_width + 2 * kv_width] / rms).astype(bf16)
        for copy in copies[count : count + 2]:
            copy.wait()
        for g in range(kv_heads):
            lanes = slice(g * HEAD_WIDTH, (g + 1) * HEAD_WIDTH)
            base = g * group * HEAD_WIDTH
            queries = jnp.concatenate(
                [
                    projected[:, base + h * HEAD_WIDTH : base + (h + 1) * HEAD_WIDTH]
                    for h in range(group)
                ],
                axis=0,
            )
            q_out[g] = queries
            key_at = query_width + g * HEAD_WIDTH
            value_at = key_at + kv_width
            new_key = projected[:, key_at : key_at + HEAD_WIDTH].astype(f32)
            new_value = projected[:, value_at : value_at + HEAD_WIDTH].astype(f32)
            new_key = jnp.concatenate([new_key] * group, axis=0)
            new_value = jnp.concatenate([new_value] * group, axis=0)
            own = jnp.sum(queries.astype(f32) * new_key, axis=1, keepdims=True) * score_scale
            own = jnp.where(first, own, very_negative)
            near = scores_of(queries, k_v[:, lanes])
            far = scores_of(queries, ks_v[:, lanes])
            far = jnp.where(bias < 0.0, very_negative, far)
            top = jnp.maximum(
                jnp.max(near, axis=1, keepdims=True), jnp.max(far, axis=1, keepdims=True)
            )
            top = jnp.maximum(top, own)
            near_weight = jnp.exp(near - top).astype(bf16)
            far_weight = jnp.where(bias < 0.0, 0.0, jnp.exp(far - top)).astype(bf16)
            own_weight = jnp.where(first, jnp.exp(own - top), 0.0).astype(bf16).astype(f32)
            if g == 0:
                for copy in copies[count + 2 :]:
                    copy.wait()
            acc = jnp.dot(near_weight, v_v[:, lanes], preferred_element_type=f32)
            acc += jnp.dot(far_weight, vs_v[:, lanes], preferred_element_type=f32)
            acc_out[g] = acc + own_weight * new_value
            denominator = (
                jnp.sum(near_weight.astype(f32), axis=1, keepdims=True)
                + jnp.sum(far_weight.astype(f32), axis=1, keepdims=True)
                + own_weight
            )
            top_out[g] = jnp.broadcast_to(top, (tall, LANES))
            sum_out[g] = jnp.broadcast_to(denominator, (tall, LANES))

    state = jax.ShapeDtypeStruct((kv_heads, tall, LANES), f32)
    return pl.pallas_call(
        kernel,
        in_specs=[ANY] * (count + 4) + [SMEM] * 2,
        out_specs=[VMEM] * 4,
        out_shape=[
            jax.ShapeDtypeStruct((kv_heads, tall, HEAD_WIDTH), bf16),
            state,
            state,
            state,
        ],
        scratch_shapes=[
            pltpu.VMEM((count, *parts[0].shape), f32),
            pltpu.VMEM(keys.shape, bf16),
            pltpu.VMEM(values.shape, bf16),
            pltpu.VMEM(suffix_keys.shape, bf16),
            pltpu.VMEM(suffix_values.shape, bf16),
            pltpu.SemaphoreType.DMA((count + 4,)),
        ],
        compiler_params=pltpu.CompilerParams(vmem_limit_bytes=32 << 20),
        cost_estimate=pl.CostEstimate(
            flops=4 * kv_heads * tall * (prefix + suffix) * HEAD_WIDTH,
            bytes_accessed=4 * (prefix + suffix) * kv_width,
            transcendentals=kv_heads * tall * (prefix + suffix),
        ),
        name="own_attention",
    )(*parts, keys, values, suffix_keys, suffix_values, lengths, assign)


def far_attention(queries, acc, top, denominator, keys, values, rows):
    kv_heads, tall, _ = queries.shape
    group = tall // rows
    heads = kv_heads * group
    count = len(keys)
    width = heads * HEAD_WIDTH

    def kernel(*refs):
        q_in, acc_in, top_in, sum_in = refs[:4]
        k_in = refs[4 : 4 + count]
        v_in = refs[4 + count : 4 + 2 * count]
        out = refs[4 + 2 * count]
        k_v, v_v, sems = refs[5 + 2 * count :]
        copies = start_copies(
            (*k_in, *v_in),
            (*(k_v.at[i] for i in range(count)), *(v_v.at[i] for i in range(count))),
            sems,
        )
        lane = lax.broadcasted_iota(jnp.int32, (rows, LANES), 1)
        stats = jnp.zeros((rows, LANES), f32)
        for copy in copies[:count]:
            copy.wait()
        for g in range(kv_heads):
            lanes = slice(g * HEAD_WIDTH, (g + 1) * HEAD_WIDTH)
            scores = [scores_of(q_in[g], k_v[i, :, lanes]) for i in range(count)]
            old_top = top_in[g]
            new_top = old_top
            for score in scores:
                new_top = jnp.maximum(new_top, jnp.max(score, axis=1, keepdims=True))
            top_high = new_top.astype(bf16).astype(f32)
            top_low = (new_top - top_high).astype(bf16).astype(f32)
            new_top = top_high + top_low
            factor = jnp.exp(old_top - new_top)
            total = acc_in[g] * factor
            weight_sum = sum_in[g] * factor
            if g == 0:
                for copy in copies[count:]:
                    copy.wait()
            for i, score in enumerate(scores):
                weight = jnp.exp(score - new_top[:, :1]).astype(bf16)
                total += jnp.dot(weight, v_v[i, :, lanes], preferred_element_type=f32)
                weight_sum += jnp.sum(weight.astype(f32), axis=1, keepdims=True)
            sum_high = weight_sum.astype(bf16).astype(f32)
            sum_low = weight_sum - sum_high
            for h in range(group):
                head = g * group + h
                part = slice(h * rows, (h + 1) * rows)
                out[:, head * HEAD_WIDTH : (head + 1) * HEAD_WIDTH] = total[part].astype(bf16)
                for k, value in enumerate((top_high, top_low, sum_high, sum_low)):
                    stats = jnp.where(lane == k * heads + head, value[part], stats)
        out[:, width:] = stats.astype(bf16)

    return pl.pallas_call(
        kernel,
        in_specs=[VMEM] * 4 + [ANY] * (2 * count),
        out_specs=VMEM,
        out_shape=jax.ShapeDtypeStruct((rows, width + LANES), bf16),
        scratch_shapes=[
            pltpu.VMEM((count, *keys[0].shape), bf16),
            pltpu.VMEM((count, *values[0].shape), bf16),
            pltpu.SemaphoreType.DMA((2 * count,)),
        ],
        compiler_params=pltpu.CompilerParams(vmem_limit_bytes=32 << 20),
        cost_estimate=pl.CostEstimate(
            flops=4 * kv_heads * tall * count * keys[0].shape[0] * HEAD_WIDTH,
            bytes_accessed=4 * count * keys[0].size,
            transcendentals=kv_heads * tall * count * keys[0].shape[0],
        ),
        name="far_attention",
    )(queries, acc, top, denominator, *keys, *values)


def combine(messages, heads):
    rows, wide = messages[0].shape
    width = wide - LANES
    count = len(messages)

    def kernel(*refs):
        message_in = refs[:count]
        out = refs[count]
        message_v, sems = refs[count + 1 :]
        copies = start_copies(message_in, [message_v.at[i] for i in range(count)], sems)
        for copy in copies:
            copy.wait()
        tops, sums = [], []
        for i in range(count):
            stats = message_v[i, :, width:].astype(f32)
            pair = stats + pltpu.roll(stats, LANES - heads, 1)
            tops.append(pair)
            sums.append(pltpu.roll(pair, LANES - 2 * heads, 1))
        top = tops[0]
        for i in range(1, count):
            top = jnp.maximum(top, tops[i])
        live = lax.broadcasted_iota(jnp.int32, (rows, LANES), 1) < heads
        factors = [jnp.where(live, jnp.exp(tops[i] - top), 0.0) for i in range(count)]
        denominator = factors[0] * sums[0]
        for i in range(1, count):
            denominator += factors[i] * sums[i]
        denominator = jnp.where(live, denominator, 1.0)
        scales = [factor / denominator for factor in factors]
        for h in range(heads):
            part = slice(h * HEAD_WIDTH, (h + 1) * HEAD_WIDTH)
            total = scales[0][:, h : h + 1] * message_v[0, :, part].astype(f32)
            for i in range(1, count):
                total += scales[i][:, h : h + 1] * message_v[i, :, part].astype(f32)
            out[:, part] = total.astype(bf16)

    return pl.pallas_call(
        kernel,
        in_specs=[ANY] * count,
        out_specs=VMEM,
        out_shape=jax.ShapeDtypeStruct((rows, width), bf16),
        scratch_shapes=[
            pltpu.VMEM((count, rows, wide), bf16),
            pltpu.SemaphoreType.DMA((count,)),
        ],
        compiler_params=pltpu.CompilerParams(vmem_limit_bytes=32 << 20),
        name="combine",
    )(*messages)


def shifted(value, axis, step):
    size = lax.axis_size(axis)
    if size & (size - 1):
        pairs = [(i, (i + step) % size) for i in range(size)]
    else:
        pairs = [(i, i ^ step) for i in range(size)]
    return lax.ppermute(value, axis, pairs)


def exchanged(value, axis):
    return [shifted(value, axis, step) for step in range(1, lax.axis_size(axis))]


def body(
    hidden,
    norm_gain,
    query_weight,
    key_matrix,
    value_matrix,
    prefix_key,
    shared_prefix_value,
    sample_suffix_key,
    sample_suffix_value,
    lengths,
    assign,
):
    rows, width = hidden.shape
    query_width = query_weight.shape[1]
    kv_width = key_matrix.shape[1]
    heads = query_width // HEAD_WIDTH
    suffix_len = sample_suffix_key.shape[1]
    direct = lax.axis_size("pfx") <= 4
    far_keys = exchanged(prefix_key, "smp")
    far_values = exchanged(shared_prefix_value, "smp")
    partial = project(hidden, norm_gain, query_weight, key_matrix, value_matrix, 4)
    if direct:
        parts = [partial] + exchanged(partial, "pfx")
    else:
        parts = [lax.psum(partial, "pfx")]
    sizes = (rows, query_width, kv_width, width * lax.axis_size("pfx"), suffix_len)
    queries, acc, top, denominator = own_attention(
        parts,
        prefix_key,
        shared_prefix_value,
        sample_suffix_key.reshape(-1, kv_width),
        sample_suffix_value.reshape(-1, kv_width),
        lengths,
        assign,
        sizes,
    )
    message = far_attention(queries, acc, top, denominator, far_keys, far_values, rows)
    if direct:
        messages = [message] + exchanged(message, "pfx")
    else:
        gathered = lax.all_gather(message, "pfx", axis=0)
        messages = [gathered[i] for i in range(lax.axis_size("pfx"))]
    return combine(messages, heads)


def solution(mesh):
    return jax.shard_map(
        body,
        mesh=mesh,
        in_specs=(
            P(("groups", "smp"), "pfx"),
            P("pfx"),
            P("pfx", "kv"),
            P("pfx", "kv"),
            P("pfx", "kv"),
            P(("groups", "pfx", "smp"), "kv"),
            P(("groups", "pfx", "smp"), "kv"),
            P(("groups", "smp"), "pfx", "kv"),
            P(("groups", "smp"), "pfx", "kv"),
            P(("groups", "smp")),
            P(("groups", "smp")),
        ),
        out_specs=P(("groups", "smp"), "kv"),
        check_vma=False,
    )
```

time: 152 us -> 43.2 us (0.28)
  blocking collectives: 58.5 us -> 0 us
  waiting for transfers between devices: 54.8 us -> 17.5 us
  between operations: 13.4 us -> 0.11 us
  starting transfers between devices: 0.13 us -> 12.3 us
  matrix products: 11.1 us -> 0 us
  Pallas kernels: 0 us -> 10.8 us
  other arithmetic: 7.82 us -> 0 us
  local copies, waits for them, and re-layouts: 5.69 us -> 2.22 us
    psum x2 -> x0, waiting for transfers between devices: 49.3 us -> none  [the longest x1 36.3 us: body(): lax.psum(block_numer.astype(jnp.bfloat16), 'pfx').astype(jnp.float32)]
    psum x2 -> x0, blocking collectives: 33.2 us -> none  [the longest x1 21.5 us: body(): lax.psum((query_part, key_part, value_part, square_part), 'pfx')]
    pmax x1 -> x0, blocking collectives: 20.4 us -> none  [body(): global_top = lax.pmax(local_top, ('pfx', 'smp'))]
    ppermute x0 -> x8, waiting for transfers between devices: none -> 17.5 us  [shifted(): return lax.ppermute(value, axis, pairs)]
    ppermute x0 -> x8, starting transfers between devices: none -> 12.3 us  [shifted(): return lax.ppermute(value, axis, pairs)]
    dot_general x13 -> x0, matrix products: 11.1 us -> none  [the longest x1 5.42 us: body(): jnp.dot(normed, query_weight, preferred_element_type=jnp.float32)]
    pallas_call x0 -> x4, Pallas kernels: none -> 10.8 us  [the longest x1 5.25 us: project(): pl.pallas_call(kernel, in_specs=[ANY] * 5, out_specs=VMEM, out_shape=jax....]
    unnamed x5 -> x0, waiting for transfers between devices: 5.3 us -> none
  transfers between devices with their start and end apart: 4 -> 8, of which waited for: 4 -> 4; matrix products, arithmetic and copies ran while one was open for 4% -> 3% of each run, Pallas kernels for 0% -> 19%
where the time goes in v1:
time: 43.2 us; the launch traced here: 43 us
  waiting for transfers between devices  17.5 us (41%)
  starting transfers between devices  12.3 us (28%)
  Pallas kernels  10.8 us (25%)
  local copies, waits for them, and re-layouts  2.22 us (5%)
    ppermute x8, waiting for transfers between devices, shifted(): return lax.ppermute(value, axis, pairs)  17.5 us
    ppermute x8, starting transfers between devices, shifted(): return lax.ppermute(value, axis, pairs)  12.3 us
    pallas_call x1, Pallas kernels, project(): pl.pallas_call(kernel, in_specs=[ANY] * 5, out_specs=VMEM, out_shape=jax....  5.25 us
    pallas_call x1, Pallas kernels, own_attention(): pl.pallas_call(kernel, in_specs=[ANY] * (count + 4) + [SMEM] * 2, out_spe...  2.98 us
    pallas_call x1, Pallas kernels, combine(): pl.pallas_call(kernel, in_specs=[ANY] * count, out_specs=VMEM, out_shape=...  1.4 us
    reshape x1, local copies, waits for them, and re-layouts, project(): norm_gain.reshape(1, width)  1.29 us
    pallas_call x1, Pallas kernels, far_attention(): pl.pallas_call(kernel, in_specs=[VMEM] * 4 + [ANY] * (2 * count), out_spe...  1.19 us
    unnamed x14, local copies, waits for them, and re-layouts  0.93 us
  transfers between devices with their start and end apart: 8, of which 4 were waited for; matrix products, arithmetic and copies ran while one was open for 3% of the time, Pallas kernels for 19%

profile of v1, /device:TPU:0, one launch (start us, length us, event | category | flops | bytes accessed | tf_op | source)
XLA Modules:
  0.0 43.0 jit_solution(28951003971720903)
XLA Ops:
  0.0 0.0 copy-start.1
  0.0 0.0 copy-start.2
  0.0 0.0 copy-start.6
  0.0 0.0 copy-start.5
  0.0 0.0 copy-start.4
  0.0 0.0 copy-start.3
  0.0 3.0 %collective-permute-start.3 = (bf16[1024,256]{1,0:T(8,128)(2,1)}, bf16[1024,256]{1,0:T(8,128)(2,1)S(1)}, u32[]{:S(2)}, u32[]{:S(2)}) collective-permute-start(bf16[1024,256]{1,0:T(8,128)(2,1)} %refs_4_.1), channel_id=1, source_target_pairs={{0,2},{2,0},{1,3},{3,1},{4,6},{6,4},{5,7},{7,5},{8,10},{10,8},{9,1... | collective-permute-start | bytes 1572872 | tf_op jit(solution)/shard_map/ppermute | solution.py:341
  3.1 0.1 collective-permute-start.4
  3.2 1.3 %reshape.9.gain_in = bf16[1,2048]{1,0:T(2,128)(2,1)} reshape(bf16[2048]{0:T(1024)(128)(2,1)} %param.12) | data formatting | bytes 8192 | tf_op jit(solution)/shard_map/reshape | solution.py:89
  4.4 5.3 %project.1.refs_0_ = f32[16,2688]{1,0:T(8,128)} custom-call(bf16[16,2048]{1,0:T(8,128)(2,1)} %hidden_in.1, bf16[1,2048]{1,0:T(2,128)(2,1)} %reshape.9.gain_in, bf16[2048,2048]{1,0:T(8,128)(2,1)} %wq_in.1, bf16[2048,256]{1,0:T(8,128)(2,1)} %wk_in.1, bf16[2048,256]{1,0:T(8,128)(2,1)} %wv_in.1), custom_call_target="tpu_custom_call" | custom-call | flops 176160768 | bytes 11010048 | tf_op jit(solution)/shard_map/project/pallas_call | solution.py:71
  9.7 4.1 %collective-permute-start.2 = (f32[16,2688]{1,0:T(8,128)}, f32[16,2688]{1,0:T(8,128)S(1)}, u32[]{:S(2)}, u32[]{:S(2)}) collective-permute-start(f32[16,2688]{1,0:T(8,128)} %project.1.refs_0_), channel_id=1, source_target_pairs={{0,12},{4,8},{8,4},{12,0},{1,13},{5,9},{9,5},{13,1},{2,14},{6,10},... | collective-permute-start | bytes 516104 | tf_op jit(solution)/shard_map/ppermute | solution.py:341
  13.8 0.0 collective-permute-start.1
  13.8 0.6 %collective-permute-start = (f32[16,2688]{1,0:T(8,128)}, f32[16,2688]{1,0:T(8,128)S(1)}, u32[]{:S(2)}, u32[]{:S(2)}) collective-permute-start(f32[16,2688]{1,0:T(8,128)} %project.1.refs_0_), channel_id=1, source_target_pairs={{0,4},{4,0},{8,12},{12,8},{1,5},{5,1},{9,13},{13,9},{2,6},{6,2},{1... | collective-permute-start | bytes 516104 | tf_op jit(solution)/shard_map/ppermute | solution.py:341
  14.5 4.8 %collective-permute-done.2.refs_3_ = f32[16,2688]{1,0:T(8,128)S(1)} collective-permute-done((f32[16,2688]{1,0:T(8,128)}, f32[16,2688]{1,0:T(8,128)S(1)}, u32[]{:S(2)}, u32[]{:S(2)}) %collective-permute-start.2) | collective-permute-done | bytes 172064 | tf_op jit(solution)/shard_map/ppermute | solution.py:341
  19.3 8.7 %collective-permute-done.1.refs_2_ = f32[16,2688]{1,0:T(8,128)S(1)} collective-permute-done((f32[16,2688]{1,0:T(8,128)}, f32[16,2688]{1,0:T(8,128)S(1)}, u32[]{:S(2)}, u32[]{:S(2)}) %collective-permute-start.1) | collective-permute-done | bytes 172064 | tf_op jit(solution)/shard_map/ppermute | solution.py:341
  28.1 0.0 collective-permute-done.refs_1_
  28.1 0.0 copy-done.1
  28.1 0.0 copy-done.2
  28.1 0.0 copy-done.6
  28.1 0.0 copy-done.5
  28.1 0.0 copy-done.4
  28.1 0.0 copy-done.3
  28.1 0.0 copy-start
  28.1 0.9 %copy-done = f32[16,2688]{1,0:T(8,128)S(1)} copy-done((f32[16,2688]{1,0:T(8,128)S(1)}, f32[16,2688]{1,0:T(8,128)}, u32[]{:S(2)}) %copy-start) | copy-done | bytes 172056
  29.0 3.0 %own_attention.1 = (bf16[2,128,128]{2,1,0:T(8,128)(2,1)S(1)}, f32[2,128,128]{2,1,0:T(8,128)S(1)}, f32[2,128,128]{2,1,0:T(8,128)S(1)}, f32[2,128,128]{2,1,0:T(8,128)S(1)}) custom-call(f32[16,2688]{1,0:T(8,128)S(1)} %copy-done, f32[16,2688]{1,0:T(8,128)S(1)} %collective-permute-done.refs_1_, f32[16,2688]{1,0:T(8,128)S(1)} %collective-permute-done.1.refs_2_, ...), custom_call_target="tpu_custom_call" | custom-call | flops 201326592 | bytes 1572864 | tf_op jit(solution)/shard_map/own_attention/pallas_call | solution.py:186
  32.0 0.0 collective-permute-done.3.refs_4_
  32.0 0.0 collective-permute-done.4.refs_5_
  32.0 1.2 %far_attention.1.refs_0_ = bf16[16,2176]{1,0:T(8,128)(2,1)S(1)} custom-call(bf16[2,128,128]{2,1,0:T(8,128)(2,1)S(1)} %get-tuple-element.9.refs_0_, f32[2,128,128]{2,1,0:T(8,128)S(1)} %get-tuple-element.10.refs_1_, f32[2,128,128]{2,1,0:T(8,128)S(1)} %get-tuple-element.11.refs_2_, f32[2,128,128]{2,1,0:T(8,128)S(1)} %get-tuple-element.12.refs_3_, ...), custom_call_target="tpu_custom_call" | custom-call | flops 134217728 | bytes 1048576 | tf_op jit(solution)/shard_map/far_attention/pallas_call | solution.py:266
  33.2 2.6 %collective-permute-start.7 = (bf16[16,2176]{1,0:T(8,128)(2,1)S(1)}, bf16[16,2176]{1,0:T(8,128)(2,1)S(1)}, u32[]{:S(2)}, u32[]{:S(2)}) collective-permute-start(bf16[16,2176]{1,0:T(8,128)(2,1)S(1)} %far_attention.1.refs_0_), channel_id=1, source_target_pairs={{0,12},{4,8},{8,4},{12,0},{1,13},{5,9},{9,5},{13,1},{2,14},{6,10},... | collective-permute-start | bytes 208904 | tf_op jit(solution)/shard_map/ppermute | solution.py:341
  35.8 0.0 collective-permute-start.6
  35.8 1.9 %collective-permute-start.5 = (bf16[16,2176]{1,0:T(8,128)(2,1)S(1)}, bf16[16,2176]{1,0:T(8,128)(2,1)S(1)}, u32[]{:S(2)}, u32[]{:S(2)}) collective-permute-start(bf16[16,2176]{1,0:T(8,128)(2,1)S(1)} %far_attention.1.refs_0_), channel_id=1, source_target_pairs={{0,4},{4,0},{8,12},{12,8},{1,5},{5,1},{9,13},{13,9},{2,6},{6,2},{1... | collective-permute-start | bytes 208904 | tf_op jit(solution)/shard_map/ppermute | solution.py:341
  37.7 2.4 %collective-permute-done.7.refs_3_ = bf16[16,2176]{1,0:T(8,128)(2,1)S(1)} collective-permute-done((bf16[16,2176]{1,0:T(8,128)(2,1)S(1)}, bf16[16,2176]{1,0:T(8,128)(2,1)S(1)}, u32[]{:S(2)}, u32[]{:S(2)}) %collective-permute-start.7) | collective-permute-done | bytes 69664 | tf_op jit(solution)/shard_map/ppermute | solution.py:341
  40.1 1.5 %collective-permute-done.6.refs_2_ = bf16[16,2176]{1,0:T(8,128)(2,1)S(1)} collective-permute-done((bf16[16,2176]{1,0:T(8,128)(2,1)S(1)}, bf16[16,2176]{1,0:T(8,128)(2,1)S(1)}, u32[]{:S(2)}, u32[]{:S(2)}) %collective-permute-start.6) | collective-permute-done | bytes 69664 | tf_op jit(solution)/shard_map/ppermute | solution.py:341
  41.6 0.0 collective-permute-done.5.refs_1_
  41.6 1.4 %combine.1 = bf16[16,2048]{1,0:T(8,128)(2,1)} custom-call(bf16[16,2176]{1,0:T(8,128)(2,1)S(1)} %far_attention.1.refs_0_, bf16[16,2176]{1,0:T(8,128)(2,1)S(1)} %collective-permute-done.5.refs_1_, bf16[16,2176]{1,0:T(8,128)(2,1)S(1)} %collective-permute-done.6.refs_2_, bf16[16,2176]{1,0:T(8,128)(2,1)S(1)} %collective-permute-done.7.refs_3_), custom_call_target="tpu_custom_call" | custom-call | tf_op jit(solution)/shard_map/combine/pallas_call | solution.py:321
Async XLA Ops:
  0.0 28.1 %copy-start.1 = (bf16[1024,256]{1,0:T(8,128)(2,1)S(1)}, bf16[1024,256]{1,0:T(8,128)(2,1)}, u32[]{:S(2)}) copy-start(bf16[1024,256]{1,0:T(8,128)(2,1)} %refs_4_.1) | copy-start | bytes 1572868
  0.0 28.1 %copy-start.2 = (bf16[1024,256]{1,0:T(8,128)(2,1)S(1)}, bf16[1024,256]{1,0:T(8,128)(2,1)}, u32[]{:S(2)}) copy-start(bf16[1024,256]{1,0:T(8,128)(2,1)} %refs_5_.1) | copy-start | bytes 1572868
  0.0 28.1 %copy-start.6 = (s32[16]{0:T(128)S(1)}, s32[16]{0:T(128)}, u32[]{:S(2)}) copy-start(s32[16]{0:T(128)} %refs_9_.1) | copy-start | bytes 196
  0.0 28.1 %copy-start.5 = (s32[16]{0:T(128)S(1)}, s32[16]{0:T(128)}, u32[]{:S(2)}) copy-start(s32[16]{0:T(128)} %refs_8_.1) | copy-start | bytes 196
  0.0 28.1 %copy-start.4 = (bf16[16,32,256]{2,1,0:T(8,128)(2,1)S(1)}, bf16[16,32,256]{2,1,0:T(8,128)(2,1)}, u32[]{:S(2)}) copy-start(bf16[16,32,256]{2,1,0:T(8,128)(2,1)} %param.19) | copy-start | bytes 786436
  0.0 28.1 %copy-start.3 = (bf16[16,32,256]{2,1,0:T(8,128)(2,1)S(1)}, bf16[16,32,256]{2,1,0:T(8,128)(2,1)}, u32[]{:S(2)}) copy-start(bf16[16,32,256]{2,1,0:T(8,128)(2,1)} %param.18) | copy-start | bytes 786436
  0.0 32.0 %collective-permute-start.3 = (bf16[1024,256]{1,0:T(8,128)(2,1)}, bf16[1024,256]{1,0:T(8,128)(2,1)S(1)}, u32[]{:S(2)}, u32[]{:S(2)}) collective-permute-start(bf16[1024,256]{1,0:T(8,128)(2,1)} %refs_4_.1), channel_id=1, source_target_pairs={{0,2},{2,0},{1,3},{3,1},{4,6},{6,4},{5,7},{7,5},{8,10},{10,8},{9,1... | collective-permute-start | bytes 1572872 | tf_op jit(solution)/shard_map/ppermute | solution.py:341
  3.1 29.0 %collective-permute-start.4 = (bf16[1024,256]{1,0:T(8,128)(2,1)}, bf16[1024,256]{1,0:T(8,128)(2,1)S(1)}, u32[]{:S(2)}, u32[]{:S(2)}) collective-permute-start(bf16[1024,256]{1,0:T(8,128)(2,1)} %refs_5_.1), channel_id=1, source_target_pairs={{0,2},{2,0},{1,3},{3,1},{4,6},{6,4},{5,7},{7,5},{8,10},{10,8},{9,1... | collective-permute-start | bytes 1572872 | tf_op jit(solution)/shard_map/ppermute | solution.py:341
  9.7 9.6 %collective-permute-start.2 = (f32[16,2688]{1,0:T(8,128)}, f32[16,2688]{1,0:T(8,128)S(1)}, u32[]{:S(2)}, u32[]{:S(2)}) collective-permute-start(f32[16,2688]{1,0:T(8,128)} %project.1.refs_0_), channel_id=1, source_target_pairs={{0,12},{4,8},{8,4},{12,0},{1,13},{5,9},{9,5},{13,1},{2,14},{6,10},... | collective-permute-start | bytes 516104 | tf_op jit(solution)/shard_map/ppermute | solution.py:341
  13.8 14.2 %collective-permute-start.1 = (f32[16,2688]{1,0:T(8,128)}, f32[16,2688]{1,0:T(8,128)S(1)}, u32[]{:S(2)}, u32[]{:S(2)}) collective-permute-start(f32[16,2688]{1,0:T(8,128)} %project.1.refs_0_), channel_id=1, source_target_pairs={{0,8},{4,12},{8,0},{12,4},{1,9},{5,13},{9,1},{13,5},{2,10},{6,14},... | collective-permute-start | bytes 516104 | tf_op jit(solution)/shard_map/ppermute | solution.py:341
  13.8 14.2 %collective-permute-start = (f32[16,2688]{1,0:T(8,128)}, f32[16,2688]{1,0:T(8,128)S(1)}, u32[]{:S(2)}, u32[]{:S(2)}) collective-permute-start(f32[16,2688]{1,0:T(8,128)} %project.1.refs_0_), channel_id=1, source_target_pairs={{0,4},{4,0},{8,12},{12,8},{1,5},{5,1},{9,13},{13,9},{2,6},{6,2},{1... | collective-permute-start | bytes 516104 | tf_op jit(solution)/shard_map/ppermute | solution.py:341
  28.1 0.9 %copy-start = (f32[16,2688]{1,0:T(8,128)S(1)}, f32[16,2688]{1,0:T(8,128)}, u32[]{:S(2)}) copy-start(f32[16,2688]{1,0:T(8,128)} %project.1.refs_0_) | copy-start | bytes 516100
  33.2 6.9 %collective-permute-start.7 = (bf16[16,2176]{1,0:T(8,128)(2,1)S(1)}, bf16[16,2176]{1,0:T(8,128)(2,1)S(1)}, u32[]{:S(2)}, u32[]{:S(2)}) collective-permute-start(bf16[16,2176]{1,0:T(8,128)(2,1)S(1)} %far_attention.1.refs_0_), channel_id=1, source_target_pairs={{0,12},{4,8},{8,4},{12,0},{1,13},{5,9},{9,5},{13,1},{2,14},{6,10},... | collective-permute-start | bytes 208904 | tf_op jit(solution)/shard_map/ppermute | solution.py:341
  35.8 5.8 %collective-permute-start.6 = (bf16[16,2176]{1,0:T(8,128)(2,1)S(1)}, bf16[16,2176]{1,0:T(8,128)(2,1)S(1)}, u32[]{:S(2)}, u32[]{:S(2)}) collective-permute-start(bf16[16,2176]{1,0:T(8,128)(2,1)S(1)} %far_attention.1.refs_0_), channel_id=1, source_target_pairs={{0,8},{4,12},{8,0},{12,4},{1,9},{5,13},{9,1},{13,5},{2,10},{6,14},... | collective-permute-start | bytes 208904 | tf_op jit(solution)/shard_map/ppermute | solution.py:341
  35.8 5.8 %collective-permute-start.5 = (bf16[16,2176]{1,0:T(8,128)(2,1)S(1)}, bf16[16,2176]{1,0:T(8,128)(2,1)S(1)}, u32[]{:S(2)}, u32[]{:S(2)}) collective-permute-start(bf16[16,2176]{1,0:T(8,128)(2,1)S(1)} %far_attention.1.refs_0_), channel_id=1, source_target_pairs={{0,4},{4,0},{8,12},{12,8},{1,5},{5,1},{9,13},{13,9},{2,6},{6,2},{1... | collective-permute-start | bytes 208904 | tf_op jit(solution)/shard_map/ppermute | solution.py:341
